TPU v7x, 32 devices: a whole 2x2x4 slice. The times are simulated.
32 devices in a mesh: shard: 8 (over y, x, core), replica: 4 (over z).
Axes of the slice: x: 2, y: 2, z: 4, core: 2. Of those that a mesh axis runs over, the one named last changes fastest.
Arguments:
- hidden: bfloat16 [8192, 768], P(('replica', 'shard')), may hold values from -6 to 6
- segment_ids: int32 [8192], P(('replica', 'shard')), may hold values from 0 to 63, as said below
- w_qkv: bfloat16 [768, 2304], P('shard'), may hold values from -0.21875 to 0.21875
- b_qv: bfloat16 [2, 768], P(None, 'shard'), may hold values from -3 to 3
- w_out: bfloat16 [768, 768], P('shard'), may hold values from -3 to 3
- b_out: bfloat16 [768], P('shard'), may hold values from -3 to 3
- gain1: bfloat16 [768], P('shard'), may hold values from 0.5 to 1.5
- shift1: bfloat16 [768], P('shard'), may hold values from -3 to 3
- w_in: bfloat16 [768, 3072], P('shard'), may hold values from -0.21875 to 0.21875
- b_in: bfloat16 [3072], P('shard'), may hold values from -3 to 3
- w_back: bfloat16 [3072, 768], P('shard'), may hold values from -0.21875 to 0.21875
- b_back: bfloat16 [768], P('shard'), may hold values from -3 to 3
- gain2: bfloat16 [768], P('shard'), may hold values from 0.5 to 1.5
- shift2: bfloat16 [768], P('shard'), may hold values from -3 to 3
- cotangent: float32 [8192, 768], P(('replica', 'shard')), may hold values from -6 to 6
Outputs:
- output: bfloat16 [8192, 768], P(('replica', 'shard'))
- d_hidden: float32 [8192, 768], P(('replica', 'shard'))
- grad_w_qkv: float32 [768, 2304], P('shard')
- grad_b_qv: float32 [2, 768], P(None, 'shard')
- grad_w_out: float32 [768, 768], P('shard')
- grad_b_out: float32 [768], P('shard')
- grad_gain1: float32 [768], P('shard')
- grad_shift1: float32 [768], P('shard')
- grad_w_in: float32 [768, 3072], P('shard')
- grad_b_in: float32 [3072], P('shard')
- grad_w_back: float32 [3072, 768], P('shard')
- grad_b_back: float32 [768], P('shard')
- grad_gain2: float32 [768], P('shard')
- grad_shift2: float32 [768], P('shard')
Inputs may be any that keep to these rules, and one draw needn't show every extreme that they name: `segment_ids`: ids never fall along the tokens. Sequence s (tokens s * 2048 to (s + 1) * 2048 - 1) holds exactly 16 documents with ids s * 16 to s * 16 + 15, one of them 1280 tokens long.
All inputs are finite; a program needn't handle non-finite values.
Results may differ from a plain program's by a relative error of at most 0.023.
Values may be sent and summed in bfloat16 or wider, within the bound.
A program may use at most 192 MiB of HBM per device.

v0:
```python
import math
import jax
import jax.numpy as jnp
from jax import lax
from jax.sharding import PartitionSpec as P

HEADS = 12
scale_factor = 0.125
norm_epsilon = 1e-05
masked_value = -1e30


def normalize(resid, gain, shift):
    mean_value = jnp.mean(resid, axis=-1, keepdims=True)
    centered = resid - mean_value
    variance = jnp.mean(centered * centered, axis=-1, keepdims=True)
    return centered * lax.rsqrt(variance + norm_epsilon) * gain + shift


def gelu_exact(values):
    return jax.nn.gelu(values, approximate=False)


def keep_state(state):
    return state


def block_size(count):
    return math.gcd(count, 512)


def masked_scores(query_heads, key_heads, query_segs, key_segs):
    scores = (
        jnp.einsum("qhd,khd->hqk", query_heads, key_heads, preferred_element_type=jnp.float32)
        * scale_factor
    )
    allowed = query_segs[:, None] == key_segs[None, :]
    return (scores, allowed[None])


def grad_block(
    query_heads, dctx_heads, log_total, delta, query_segs, key_heads, value_heads, key_segs
):
    scores, allowed = masked_scores(query_heads, key_heads, query_segs, key_segs)
    probs = jnp.where(allowed, jnp.exp(scores - log_total[:, :, None]), 0.0)
    d_prob = jnp.einsum("qhd,khd->hqk", dctx_heads, value_heads, preferred_element_type=jnp.float32)
    d_scores = (probs * (d_prob - delta[:, :, None])).astype(jnp.bfloat16)
    return (probs.astype(jnp.bfloat16), d_scores)


def body(
    hidden,
    segment_ids,
    w_qkv,
    b_qv,
    w_out,
    b_out,
    gain1,
    shift1,
    w_in,
    b_in,
    w_back,
    b_back,
    gain2,
    shift2,
    cotangent,
):
    tok_rows, width = hidden.shape
    heads = HEADS
    head_dim = width // heads
    seg_low = segment_ids[0]
    seg_high = segment_ids[-1]
    wq_full, wo_full, bqv_full, bo_full, g1_full, s1_full = (
        lax.all_gather(w_qkv, "shard", axis=0, tiled=True),
        lax.all_gather(w_out, "shard", axis=0, tiled=True),
        lax.all_gather(b_qv, "shard", axis=1, tiled=True),
        lax.all_gather(b_out, "shard", axis=0, tiled=True),
        lax.all_gather(gain1, "shard", axis=0, tiled=True),
        lax.all_gather(shift1, "shard", axis=0, tiled=True),
    )
    qkv = jnp.dot(hidden, wq_full, preferred_element_type=jnp.float32)
    bqv_wide = bqv_full.astype(jnp.float32)
    query = (qkv[:, :width] + bqv_wide[0]).astype(jnp.bfloat16)
    keys = qkv[:, width : 2 * width].astype(jnp.bfloat16)
    values = (qkv[:, 2 * width :] + bqv_wide[1]).astype(jnp.bfloat16)
    query_heads = query.reshape(tok_rows, heads, head_dim)
    key_local = keys.reshape(tok_rows, heads, head_dim)
    value_local = values.reshape(tok_rows, heads, head_dim)
    start_state = (
        jnp.full((heads, tok_rows), masked_value, jnp.float32),
        jnp.zeros((heads, tok_rows), jnp.float32),
        jnp.zeros((tok_rows, heads, head_dim), jnp.float32),
    )
    key_piece = lax.all_gather(keys, "shard", axis=0, tiled=True)
    value_piece = lax.all_gather(values, "shard", axis=0, tiled=True)
    seg_piece = lax.all_gather(segment_ids, "shard", axis=0, tiled=True)
    count = key_piece.shape[0]
    block = block_size(count)

    def forward_step(index, state):
        offset = index * block
        key_heads = lax.dynamic_slice_in_dim(key_piece, offset, block, 0).reshape(
            block, heads, head_dim
        )
        value_heads = lax.dynamic_slice_in_dim(value_piece, offset, block, 0).reshape(
            block, heads, head_dim
        )
        key_segs = lax.dynamic_slice_in_dim(seg_piece, offset, block, 0)

        def forward_update(state):
            running_max, running_sum, accum = state
            scores, allowed = masked_scores(query_heads, key_heads, segment_ids, key_segs)
            new_max = jnp.maximum(
                running_max, jnp.max(jnp.where(allowed, scores, masked_value), axis=-1)
            )
            factor = jnp.exp(running_max - new_max)
            weights = jnp.where(allowed, jnp.exp(scores - new_max[:, :, None]), 0.0)
            running_sum = running_sum * factor + jnp.sum(weights, axis=-1)
            accum = accum * factor.T[:, :, None] + jnp.einsum(
                "hqk,khd->qhd",
                weights.astype(jnp.bfloat16),
                value_heads,
                preferred_element_type=jnp.float32,
            )
            return (new_max, running_sum, accum)

        touches = jnp.logical_and(key_segs[0] <= seg_high, key_segs[-1] >= seg_low)
        return lax.cond(touches, forward_update, keep_state, state)

    running_max, running_sum, accum = lax.fori_loop(0, count // block, forward_step, start_state)
    context32 = accum / running_sum.T[:, :, None]
    log_total = running_max + jnp.log(running_sum)
    context = context32.reshape(tok_rows, width).astype(jnp.bfloat16)
    resid1 = (
        hidden.astype(jnp.float32)
        + jnp.dot(context, wo_full, preferred_element_type=jnp.float32)
        + bo_full.astype(jnp.float32)
    )
    normed1, norm1_pull = jax.vjp(
        normalize, resid1, g1_full.astype(jnp.float32), s1_full.astype(jnp.float32)
    )
    wi_full, bi_full, wb_full, bb_full, g2_full, s2_full = (
        lax.all_gather(w_in, "shard", axis=0, tiled=True),
        lax.all_gather(b_in, "shard", axis=0, tiled=True),
        lax.all_gather(w_back, "shard", axis=0, tiled=True),
        lax.all_gather(b_back, "shard", axis=0, tiled=True),
        lax.all_gather(gain2, "shard", axis=0, tiled=True),
        lax.all_gather(shift2, "shard", axis=0, tiled=True),
    )
    normed1_low = normed1.astype(jnp.bfloat16)
    pre = jnp.dot(normed1_low, wi_full, preferred_element_type=jnp.float32) + bi_full.astype(
        jnp.float32
    )
    act, gelu_pull = jax.vjp(gelu_exact, pre)
    act_low = act.astype(jnp.bfloat16)
    resid2 = (
        normed1
        + jnp.dot(act_low, wb_full, preferred_element_type=jnp.float32)
        + bb_full.astype(jnp.float32)
    )
    out32, norm2_pull = jax.vjp(
        normalize, resid2, g2_full.astype(jnp.float32), s2_full.astype(jnp.float32)
    )
    output = out32.astype(jnp.bfloat16)
    d_resid2, grad_gain2, grad_shift2 = norm2_pull(cotangent)
    d_branch2 = d_resid2.astype(jnp.bfloat16)
    grad_b_back = jnp.sum(d_resid2, axis=0)
    grad_w_back = jnp.einsum("tf,td->fd", act_low, d_branch2, preferred_element_type=jnp.float32)
    d_act = jnp.einsum("td,fd->tf", d_branch2, wb_full, preferred_element_type=jnp.float32)
    (d_pre,) = gelu_pull(d_act)
    grad_b_in = jnp.sum(d_pre, axis=0)
    d_pre_low = d_pre.astype(jnp.bfloat16)
    grad_w_in = jnp.einsum("td,tf->df", normed1_low, d_pre_low, preferred_element_type=jnp.float32)
    d_normed1 = d_resid2 + jnp.einsum(
        "tf,df->td", d_pre_low, wi_full, preferred_element_type=jnp.float32
    )
    d_resid1, grad_gain1, grad_shift1 = norm1_pull(d_normed1)
    grad_b_out = jnp.sum(d_resid1, axis=0)
    d_branch1 = d_resid1.astype(jnp.bfloat16)
    grad_w_out = jnp.einsum("tc,td->cd", context, d_branch1, preferred_element_type=jnp.float32)
    d_context = jnp.einsum(
        "td,cd->tc", d_branch1, wo_full, preferred_element_type=jnp.float32
    ).astype(jnp.bfloat16)
    dctx_heads = d_context.reshape(tok_rows, heads, head_dim)
    delta = jnp.einsum("qhd,qhd->hq", dctx_heads.astype(jnp.float32), context32)
    zero_heads = jnp.zeros((tok_rows, heads, head_dim), jnp.float32)
    query_key_piece = lax.all_gather(keys, "shard", axis=0, tiled=True)
    query_value_piece = lax.all_gather(values, "shard", axis=0, tiled=True)
    query_seg_piece = lax.all_gather(segment_ids, "shard", axis=0, tiled=True)
    count = query_key_piece.shape[0]
    query_block = block_size(count)

    def query_step(index, summed):
        offset = index * query_block
        key_heads = lax.dynamic_slice_in_dim(query_key_piece, offset, query_block, 0).reshape(
            query_block, heads, head_dim
        )
        value_heads = lax.dynamic_slice_in_dim(query_value_piece, offset, query_block, 0).reshape(
            query_block, heads, head_dim
        )
        key_segs = lax.dynamic_slice_in_dim(query_seg_piece, offset, query_block, 0)

        def query_update(summed):
            probs, d_scores = grad_block(
                query_heads,
                dctx_heads,
                log_total,
                delta,
                segment_ids,
                key_heads,
                value_heads,
                key_segs,
            )
            return (
                summed
                + jnp.einsum(
                    "hqk,khd->qhd", d_scores, key_heads, preferred_element_type=jnp.float32
                )
                * scale_factor
            )

        touches = jnp.logical_and(key_segs[0] <= seg_high, key_segs[-1] >= seg_low)
        return lax.cond(touches, query_update, keep_state, summed)

    d_query = lax.fori_loop(0, count // query_block, query_step, zero_heads)
    all_log_total, all_delta = (
        lax.all_gather(log_total, "shard", axis=1, tiled=True),
        lax.all_gather(delta, "shard", axis=1, tiled=True),
    )
    query_piece = lax.all_gather(query, "shard", axis=0, tiled=True)
    dctx_piece = lax.all_gather(d_context, "shard", axis=0, tiled=True)
    key_seg_piece = lax.all_gather(segment_ids, "shard", axis=0, tiled=True)
    count = query_piece.shape[0]
    key_block = block_size(count)

    def key_step(index, state):
        offset = index * key_block
        piece_query = lax.dynamic_slice_in_dim(query_piece, offset, key_block, 0).reshape(
            key_block, heads, head_dim
        )
        piece_dctx = lax.dynamic_slice_in_dim(dctx_piece, offset, key_block, 0).reshape(
            key_block, heads, head_dim
        )
        piece_segs = lax.dynamic_slice_in_dim(key_seg_piece, offset, key_block, 0)
        piece_log = lax.dynamic_slice_in_dim(all_log_total, offset, key_block, 1)
        piece_delta = lax.dynamic_slice_in_dim(all_delta, offset, key_block, 1)

        def key_update(state):
            d_key, d_value = state
            probs, d_scores = grad_block(
                piece_query,
                piece_dctx,
                piece_log,
                piece_delta,
                piece_segs,
                key_local,
                value_local,
                segment_ids,
            )
            d_key = (
                d_key
                + jnp.einsum(
                    "hqk,qhd->khd", d_scores, piece_query, preferred_element_type=jnp.float32
                )
                * scale_factor
            )
            d_value = d_value + jnp.einsum(
                "hqk,qhd->khd", probs, piece_dctx, preferred_element_type=jnp.float32
            )
            return (d_key, d_value)

        touches = jnp.logical_and(piece_segs[0] <= seg_high, piece_segs[-1] >= seg_low)
        return lax.cond(touches, key_update, keep_state, state)

    d_key_heads, d_value_heads = lax.fori_loop(
        0, count // key_block, key_step, (zero_heads, zero_heads)
    )
    d_keys = d_key_heads.reshape(tok_rows, width)
    d_values = d_value_heads.reshape(tok_rows, width)
    d_query = d_query.reshape(tok_rows, width)
    grad_b_qv = jnp.stack([jnp.sum(d_query, axis=0), jnp.sum(d_values, axis=0)], axis=0)
    d_qkv = jnp.concatenate([d_query, d_keys, d_values], axis=1).astype(jnp.bfloat16)
    grad_w_qkv = jnp.einsum("td,te->de", hidden, d_qkv, preferred_element_type=jnp.float32)
    d_hidden = d_resid1 + jnp.einsum(
        "te,de->td", d_qkv, wq_full, preferred_element_type=jnp.float32
    )
    local_grads = (
        grad_w_qkv,
        grad_b_qv,
        grad_w_out,
        grad_b_out,
        grad_gain1,
        grad_shift1,
        grad_w_in,
        grad_b_in,
        grad_w_back,
        grad_b_back,
        grad_gain2,
        grad_shift2,
    )
    shard_grads = (
        lax.psum_scatter(
            local_grads[0].astype(jnp.bfloat16), "shard", scatter_dimension=0, tiled=True
        ).astype(jnp.float32),
        lax.psum_scatter(
            local_grads[1].astype(jnp.bfloat16), "shard", scatter_dimension=1, tiled=True
        ).astype(jnp.float32),
        lax.psum_scatter(
            local_grads[2].astype(jnp.bfloat16), "shard", scatter_dimension=0, tiled=True
        ).astype(jnp.float32),
        lax.psum_scatter(
            local_grads[3].astype(jnp.bfloat16), "shard", scatter_dimension=0, tiled=True
        ).astype(jnp.float32),
        lax.psum_scatter(
            local_grads[4].astype(jnp.bfloat16), "shard", scatter_dimension=0, tiled=True
        ).astype(jnp.float32),
        lax.psum_scatter(
            local_grads[5].astype(jnp.bfloat16), "shard", scatter_dimension=0, tiled=True
        ).astype(jnp.float32),
        lax.psum_scatter(
            local_grads[6].astype(jnp.bfloat16), "shard", scatter_dimension=0, tiled=True
        ).astype(jnp.float32),
        lax.psum_scatter(
            local_grads[7].astype(jnp.bfloat16), "shard", scatter_dimension=0, tiled=True
        ).astype(jnp.float32),
        lax.psum_scatter(
            local_grads[8].astype(jnp.bfloat16), "shard", scatter_dimension=0, tiled=True
        ).astype(jnp.float32),
        lax.psum_scatter(
            local_grads[9].astype(jnp.bfloat16), "shard", scatter_dimension=0, tiled=True
        ).astype(jnp.float32),
        lax.psum_scatter(
            local_grads[10].astype(jnp.bfloat16), "shard", scatter_dimension=0, tiled=True
        ).astype(jnp.float32),
        lax.psum_scatter(
            local_grads[11].astype(jnp.bfloat16), "shard", scatter_dimension=0, tiled=True
        ).astype(jnp.float32),
    )
    total_grads = (
        lax.psum(shard_grads[0].astype(jnp.bfloat16), "replica").astype(jnp.float32),
        lax.psum(shard_grads[1].astype(jnp.bfloat16), "replica").astype(jnp.float32),
        lax.psum(shard_grads[2].astype(jnp.bfloat16), "replica").astype(jnp.float32),
        lax.psum(shard_grads[3].astype(jnp.bfloat16), "replica").astype(jnp.float32),
        lax.psum(shard_grads[4].astype(jnp.bfloat16), "replica").astype(jnp.float32),
        lax.psum(shard_grads[5].astype(jnp.bfloat16), "replica").astype(jnp.float32),
        lax.psum(shard_grads[6].astype(jnp.bfloat16), "replica").astype(jnp.float32),
        lax.psum(shard_grads[7].astype(jnp.bfloat16), "replica").astype(jnp.float32),
        lax.psum(shard_grads[8].astype(jnp.bfloat16), "replica").astype(jnp.float32),
        lax.psum(shard_grads[9].astype(jnp.bfloat16), "replica").astype(jnp.float32),
        lax.psum(shard_grads[10].astype(jnp.bfloat16), "replica").astype(jnp.float32),
        lax.psum(shard_grads[11].astype(jnp.bfloat16), "replica").astype(jnp.float32),
    )
    return (output, d_hidden) + tuple(total_grads)


def solution(mesh):
    in_specs = (
        P(("replica", "shard"), None),
        P(("replica", "shard")),
        P("shard", None),
        P(None, "shard"),
        P("shard", None),
        P("shard"),
        P("shard"),
        P("shard"),
        P("shard", None),
        P("shard"),
        P("shard", None),
        P("shard"),
        P("shard"),
        P("shard"),
        P(("replica", "shard"), None),
    )
    out_specs = (
        P(("replica", "shard"), None),
        P(("replica", "shard"), None),
        P("shard", None),
        P(None, "shard"),
        P("shard", None),
        P("shard"),
        P("shard"),
        P("shard"),
        P("shard", None),
        P("shard"),
        P("shard", None),
        P("shard"),
        P("shard"),
        P("shard"),
    )
    return jax.shard_map(body, mesh=mesh, in_specs=in_specs, out_specs=out_specs, check_vma=False)
```

profile of v0, /device:TPU:0, one launch (start us, length us, event | category | flops | bytes accessed | tf_op | source)
XLA Modules:
  0.0 788.4 jit_solution(2066285224074038387)
XLA Ops:
  8.0 38.5 %all-gather.12.cloned.1.call-done = bf16[768,2304]{1,0:T(8,128)(2,1)} async-done(((bf16[96,2304]{1,0:T(8,128)(2,1)}), bf16[768,2304]{1,0:T(8,128)(2,1)}) %all-gather.12.cloned.1.call-update) | async-done | bytes 3538960 | tf_op jit(solution)/shard_map/all_gather | solution.py:74
  64.7 24.2 %all-reduce.14 = (bf16[768]{0:T(1024)(128)(2,1)S(1)}, bf16[768]{0:T(1024)(128)(2,1)S(1)}, bf16[768]{0:T(1024)(128)(2,1)S(1)}, bf16[768]{0:T(1024)(128)(2,1)S(1)}, bf16[768]{0:T(1024)(128)(2,1)S(1)}) all-reduce(bf16[768]{0:T(1024)(128)(2,1)S(1)} %dynamic-update-slice, ...), channel_id=1, replica_groups=mesh['shard'=8,'replica'=4] {'shard'}, use_global_device_ids=true, to_apply=%add | all-reduce | flops 3840 | bytes 15360
  97.0 8.8 %all-gather = s32[8,1,256]{2,1,0:T(1,128)} all-gather(s32[1,1,256]{2,1,0:T(1,128)S(1)} %bitcast.168), channel_id=1, replica_groups=mesh['shard'=8,'replica'=4] {'shard'}, dimensions={0}, use_global_device_ids=true | all-gather | bytes 9216 | tf_op jit(solution)/shard_map/all_gather | solution.py:96
  122.7 32.9 %while.48 = (s32[]{:T(128)}, f32[12,256]{1,0:T(8,128)S(1)}, f32[12,256]{1,0:T(8,128)S(1)}, f32[256,12,64]{0,2,1:T(8,128)S(1)}, s32[2048]{0:T(1024)}, /*index=5*/...) while((s32[]{:T(128)}, f32[12,256]{1,0:T(8,128)S(1)}, ...), condition=%wide.region_5.6_spmd, body=%wide.region_0.5_spmd.sunk | while | flops 420488192 | bytes 26287476 | solution.py:130
  158.3 25.8 %all-gather.20.cloned.1.call-done = bf16[768,3072]{1,0:T(8,128)(2,1)} async-done(((bf16[96,3072]{1,0:T(8,128)(2,1)}), bf16[768,3072]{1,0:T(8,128)(2,1)}) %all-gather.20.cloned.1.call-update) | async-done | bytes 4718608 | tf_op jit(solution)/shard_map/all_gather | solution.py:143
  184.0 12.1 %multiply_convert_fusion.8 = (bf16[256,3072]{1,0:T(8,128)(2,1)}, f32[256,3072]{1,0:T(8,128)}, f32[256,3072]{1,0:T(8,128)}) fusion(f32[3072]{0:T(1024)S(1)} %bitcast.171, bf16[768,3072]{1,0:T(8,128)(2,1)} %all-gather.20.cloned.1.call-done, f32[256,768]{1,0:T(8,128)S(1)} %get-tuple-element.1246, f32[768]{0:T(1024)S(1)} %convert_element_type.209, ...), kind=kOutput, calls=%fused_computation.63 | convolution fusion | flops 1260847104 | bytes 13389824 | tf_op jit(solution)/shard_map/dot_general | solution.py:151
  196.1 28.4 %all-gather.22.cloned.1.call-done = bf16[3072,768]{1,0:T(8,128)(2,1)} async-done(((bf16[384,768]{1,0:T(8,128)(2,1)}), bf16[3072,768]{1,0:T(8,128)(2,1)}) %all-gather.22.cloned.1.call-update) | async-done | bytes 4718608 | tf_op jit(solution)/shard_map/all_gather | solution.py:145
  242.4 16.2 %all-gather.24.cloned.1.call-done = bf16[2048,768]{1,0:T(8,128)(2,1)} async-done(((bf16[256,768]{1,0:T(8,128)(2,1)}), bf16[2048,768]{1,0:T(8,128)(2,1)}) %all-gather.24.cloned.1.call-update) | async-done | bytes 3145744 | tf_op jit(solution)/shard_map/all_gather | solution.py:230
  264.1 9.3 %all_gather.77 = f32[12,2048]{1,0:T(8,128)S(1)} all-gather(f32[12,256]{1,0:T(8,128)} %log_add_fusion), channel_id=1, replica_groups=mesh['shard'=8,'replica'=4] {'shard'}, dimensions={1}, use_global_device_ids=true | all-gather | bytes 110592 | tf_op jit(solution)/shard_map/all_gather | solution.py:227
  284.6 51.7 %while.49 = (s32[]{:T(128)}, f32[256,12,64]{0,2,1:T(8,128)}, s32[2048]{0:T(1024)}, s32[]{:T(128)}, s32[]{:T(128)}, /*index=5*/s32[256]{0:T(256)}, bf16[2048,768]...) while((s32[]{:T(128)}, f32[256,12,64]{0,2,1:T(8,128)}, ...), condition=%wide.region_17.18_spmd, body=%wide.region_14.17_spmd.sunk | while | flops 613941248 | bytes 20745584 | solution.py:225
  288.8 11.8 %conditional.7 = (f32[256,12,64]{0,2,1:T(8,128)}) conditional(s32[]{:T(128)} %convert_element_type.315, f32[256,12,64]{0,2,1:T(8,128)} %get-tuple-element.1570, (s32[256]{0:T(256)}, s32[512]{0:T(512)S(1)}, bf16[2048,768]{0,1:T(8,128)(2,1)}, s32[]{:T(128)}, bf16[256,12,64]{0,2,1:T(8,128)(2,1)S(1)}, /*index=5*/f32[12,256]{1,0:T(8,128)}, ...), branch_computations={%region_15.15_spmd, %region_16.16_spmd} | conditional | flops 613941248 | bytes 20741160 | solution.py:223
  304.7 11.8 %conditional.7 = (f32[256,12,64]{0,2,1:T(8,128)}) conditional(s32[]{:T(128)} %convert_element_type.315, f32[256,12,64]{0,2,1:T(8,128)} %get-tuple-element.1570, (s32[256]{0:T(256)}, s32[512]{0:T(512)S(1)}, bf16[2048,768]{0,1:T(8,128)(2,1)}, s32[]{:T(128)}, bf16[256,12,64]{0,2,1:T(8,128)(2,1)S(1)}, /*index=5*/f32[12,256]{1,0:T(8,128)}, ...), branch_computations={%region_15.15_spmd, %region_16.16_spmd} | conditional | flops 613941248 | bytes 20741160 | solution.py:223
  320.5 11.8 %conditional.7 = (f32[256,12,64]{0,2,1:T(8,128)}) conditional(s32[]{:T(128)} %convert_element_type.315, f32[256,12,64]{0,2,1:T(8,128)} %get-tuple-element.1570, (s32[256]{0:T(256)}, s32[512]{0:T(512)S(1)}, bf16[2048,768]{0,1:T(8,128)(2,1)}, s32[]{:T(128)}, bf16[256,12,64]{0,2,1:T(8,128)(2,1)S(1)}, /*index=5*/f32[12,256]{1,0:T(8,128)}, ...), branch_computations={%region_15.15_spmd, %region_16.16_spmd} | conditional | flops 613941248 | bytes 20741160 | solution.py:223
  342.9 66.5 %while.50 = (s32[]{:T(128)}, f32[256,12,64]{0,2,1:T(8,128)}, f32[256,12,64]{0,2,1:T(8,128)}, s32[2048]{0:T(1024)}, s32[]{:T(128)}, /*index=5*/s32[]{:T(128)}, s3...) while((s32[]{:T(128)}, f32[256,12,64]{0,2,1:T(8,128)}, ...), condition=%wide.region_21.22_spmd, body=%wide.region_18.21_spmd.sunk | while | flops 821755904 | bytes 29670792 | solution.py:275
  346.9 16.9 %conditional.8 = ((f32[256,12,64]{0,2,1:T(8,128)}, f32[256,12,64]{0,2,1:T(8,128)})) conditional(s32[]{:T(128)} %convert_element_type.316, (f32[256,12,64]{0,2,1:T(8,128)}, f32[256,12,64]{0,2,1:T(8,128)}) %tuple.174, (s32[512]{0:T(512)S(1)}, s32[256]{0:T(256)S(1)}, bf16[2048,768]{0,1:T(8,128)(2,1)}, s32[]{:T(128)}, ...), branch_computations={%region_19.19_spmd, %region_20.20_spmd} | conditional | flops 821755904 | bytes 29666336 | solution.py:273
  367.7 16.9 %conditional.8 = ((f32[256,12,64]{0,2,1:T(8,128)}, f32[256,12,64]{0,2,1:T(8,128)})) conditional(s32[]{:T(128)} %convert_element_type.316, (f32[256,12,64]{0,2,1:T(8,128)}, f32[256,12,64]{0,2,1:T(8,128)}) %tuple.174, (s32[512]{0:T(512)S(1)}, s32[256]{0:T(256)S(1)}, bf16[2048,768]{0,1:T(8,128)(2,1)}, s32[]{:T(128)}, ...), branch_computations={%region_19.19_spmd, %region_20.20_spmd} | conditional | flops 821755904 | bytes 29666336 | solution.py:273
  388.6 16.9 %conditional.8 = ((f32[256,12,64]{0,2,1:T(8,128)}, f32[256,12,64]{0,2,1:T(8,128)})) conditional(s32[]{:T(128)} %convert_element_type.316, (f32[256,12,64]{0,2,1:T(8,128)}, f32[256,12,64]{0,2,1:T(8,128)}) %tuple.174, (s32[512]{0:T(512)S(1)}, s32[256]{0:T(256)S(1)}, bf16[2048,768]{0,1:T(8,128)(2,1)}, s32[]{:T(128)}, ...), branch_computations={%region_19.19_spmd, %region_20.20_spmd} | conditional | flops 821755904 | bytes 29666336 | solution.py:273
  440.5 58.1 %reduce-scatter.16.cloned.1.call-done = bf16[96,2304]{1,0:T(8,128)(2,1)} async-done(((bf16[768,2304]{1,0:T(8,128)(2,1)}), bf16[96,2304]{1,0:T(8,128)(2,1)}) %reduce-scatter.16.cloned.1.call-update) | async-done | bytes 442384
  500.8 38.3 %reduce-scatter.10.cloned.1.call-done = bf16[96,768]{1,0:T(8,128)(2,1)} async-done(((bf16[768,768]{1,0:T(8,128)(2,1)}), bf16[96,768]{1,0:T(8,128)(2,1)}) %reduce-scatter.10.cloned.1.call-update) | async-done | bytes 147472 | tf_op jit(solution)/shard_map/reduce_scatter | solution.py:308
  539.1 57.3 %reduce-scatter.12.cloned.1.call-done = bf16[96,3072]{1,0:T(8,128)(2,1)} async-done(((bf16[768,3072]{1,0:T(8,128)(2,1)}), bf16[96,3072]{1,0:T(8,128)(2,1)}) %reduce-scatter.12.cloned.1.call-update) | async-done | bytes 589840 | tf_op jit(solution)/shard_map/reduce_scatter | solution.py:320
  596.3 57.1 %reduce-scatter.14.cloned.1.call-done = bf16[384,768]{1,0:T(8,128)(2,1)} async-done(((bf16[3072,768]{1,0:T(8,128)(2,1)}), bf16[384,768]{1,0:T(8,128)(2,1)}) %reduce-scatter.14.cloned.1.call-update) | async-done | bytes 589840 | tf_op jit(solution)/shard_map/reduce_scatter | solution.py:326
  658.2 23.6 %all-reduce.13 = (bf16[768]{0:T(1024)(128)(2,1)S(1)}, bf16[768]{0:T(1024)(128)(2,1)S(1)}, bf16[768]{0:T(1024)(128)(2,1)S(1)}, bf16[768]{0:T(1024)(128)(2,1)S(1)}...) all-reduce(bf16[768]{0:T(1024)(128)(2,1)} %dynamic-update-slice.5, ...), channel_id=1, replica_groups=mesh['shard'=8,'replica'=4] {'shard'}, use_global_device_ids=true, to_apply=%add.5 | all-reduce | flops 8448 | bytes 33792
  691.5 11.9 %all-reduce.15 = (bf16[2,96]{1,0:T(2,128)(2,1)S(1)}, bf16[96]{0:T(256)(128)(2,1)S(1)}, bf16[96]{0:T(256)(128)(2,1)S(1)}, bf16[96]{0:T(256)(128)(2,1)S(1)}, bf16[...) all-reduce(bf16[2,96]{1,0:T(2,128)(2,1)S(1)} %copy.95, ...), channel_id=1, replica_groups=mesh['shard'=8,'replica'=4] {'replica'}, use_global_device_ids=true, to_apply=%region_27.28 | all-reduce | flops 1152 | bytes 4608 | tf_op jit(solution)/shard_map/psum | solution.py:341
  707.7 66.8 %all-reduce.19.cloned.1.call-done = (bf16[96,2304]{0,1:T(8,128)(2,1)}, bf16[96,768]{1,0:T(8,128)(2,1)}, bf16[96,3072]{1,0:T(8,128)(2,1)}, bf16[384,768]{1,0:T(8,128)(2,1)}) async-done(((bf16[96,2304]{0,1:T(8,128)(2,1)}, bf16[96,768]{1,0:T(8,128)(2,1)}, bf16[96,3072]{1,0:T(8,128)(2,1)}, bf16[384,768]{1,0:T(8,128)(2,1)}), (bf16[96,2304]{0,1:T(8,128)(2,1)}, bf16[96,768]{1,0:T(8,128)(2,1)}, ...) | async-done | bytes 1769488 | tf_op jit(solution)/shard_map/psum | solution.py:340
  (333 shorter events, 280.0 us)
Async XLA Ops:
  7.2 39.3 %all-gather.12.cloned.1.call-start = ((), (), s32[]{:S(2)}) async-start(), calls=%async_computation.5 | async-start | bytes 3981312 | tf_op jit(solution)/shard_map/all_gather | solution.py:74
  7.9 99.1 %all-gather.14.cloned.1.call-start = ((), (), s32[]{:S(2)}) async-start(), calls=%async_computation.6 | async-start | bytes 3538944 | tf_op jit(solution)/shard_map/all_gather | solution.py:94
  49.8 47.2 %copy-start.20 = (s32[256]{0:T(256)S(1)}, s32[256]{0:T(256)}, u32[]{:S(2)}) copy-start(s32[256]{0:T(256)} %param.28) | copy-start | bytes 3076
  50.6 67.2 %all-gather.16.cloned.1.call-start = ((), (), s32[]{:S(2)}) async-start(), calls=%async_computation.7 | async-start | bytes 3538944 | tf_op jit(solution)/shard_map/all_gather | solution.py:95
  60.4 95.2 %all-gather.18.cloned.1.call-start = ((), (), s32[]{:S(2)}) async-start(), calls=%async_computation.8 | async-start | bytes 1327104 | tf_op jit(solution)/shard_map/all_gather | solution.py:75
  61.0 123.0 %all-gather.20.cloned.1.call-start = ((), (), s32[]{:S(2)}) async-start(), calls=%async_computation.9 | async-start | bytes 5308416 | tf_op jit(solution)/shard_map/all_gather | solution.py:143
  61.6 163.0 %all-gather.22.cloned.1.call-start = ((), (), s32[]{:S(2)}) async-start(), calls=%async_computation.10 | async-start | bytes 5308416 | tf_op jit(solution)/shard_map/all_gather | solution.py:145
  62.2 196.5 %all-gather.24.cloned.1.call-start = ((), (), s32[]{:S(2)}) async-start(), calls=%async_computation.11 | async-start | bytes 3538944 | tf_op jit(solution)/shard_map/all_gather | solution.py:230
  97.0 127.6 %copy-start.25 = (f32[768]{0:T(1024)}, f32[768]{0:T(1024)S(1)}, u32[]{:S(2)}) copy-start(f32[768]{0:T(1024)S(1)} %convert_element_type.209) | copy-start | bytes 9220
  97.0 139.6 %copy-start.23 = (f32[768]{0:T(1024)}, f32[768]{0:T(1024)S(1)}, u32[]{:S(2)}) copy-start(f32[768]{0:T(1024)S(1)} %convert_element_type.208) | copy-start | bytes 9220
  97.0 133.3 %copy-start.27 = (f32[768]{0:T(1024)}, f32[768]{0:T(1024)S(1)}, u32[]{:S(2)}) copy-start(f32[768]{0:T(1024)S(1)} %convert_element_type.214) | copy-start | bytes 9220
  106.7 229.7 %all-gather.26.cloned.1.call-start = ((), (), s32[]{:S(2)}) async-start(), calls=%async_computation.12 | async-start | bytes 3538944 | tf_op jit(solution)/shard_map/all_gather | solution.py:231
  158.0 78.6 %copy-start.31 = (f32[256]{0:T(256)}, f32[256]{0:T(256)S(1)}, u32[]{:S(2)}) copy-start(f32[256]{0:T(256)S(1)} %broadcast_multiply_fusion.1) | copy-start | bytes 3076
  158.3 78.4 %copy-start.36 = (f32[256]{0:T(256)}, f32[256]{0:T(256)S(1)}, u32[]{:S(2)}) copy-start(f32[256]{0:T(256)S(1)} %fusion.71) | copy-start | bytes 3076
  238.3 260.4 %reduce-scatter.16.cloned.1.call-start = ((), (), s32[]{:S(2)}) async-start(), calls=%async_computation.16 | async-start | bytes 3981312
  422.3 116.8 %reduce-scatter.10.cloned.1.call-start = ((), (), s32[]{:S(2)}) async-start(), calls=%async_computation.13 | async-start | bytes 1327104 | tf_op jit(solution)/shard_map/reduce_scatter | solution.py:308
  425.1 171.3 %reduce-scatter.12.cloned.1.call-start = ((), (), s32[]{:S(2)}) async-start(), calls=%async_computation.14 | async-start | bytes 5308416 | tf_op jit(solution)/shard_map/reduce_scatter | solution.py:320
  430.5 222.9 %reduce-scatter.14.cloned.1.call-start = ((), (), s32[]{:S(2)}) async-start(), calls=%async_computation.15 | async-start | bytes 5308416 | tf_op jit(solution)/shard_map/reduce_scatter | solution.py:326
  436.7 245.6 %copy-start.1 = (f32[256,768]{1,0:T(8,128)S(1)}, f32[256,768]{1,0:T(8,128)}, u32[]{:S(2)}) copy-start(f32[256,768]{1,0:T(8,128)} %copy-done) | copy-start | bytes 2359300
  436.7 245.6 %copy-start.28 = (f32[768]{0:T(1024)S(1)}, f32[768]{0:T(1024)}, u32[]{:S(2)}) copy-start(f32[768]{0:T(1024)} %copy-done.27) | copy-start | bytes 9220
  436.8 245.6 %copy-start.30 = (f32[256]{0:T(256)S(1)}, f32[256]{0:T(256)}, u32[]{:S(2)}) copy-start(f32[256]{0:T(256)} %copy-done.29) | copy-start | bytes 3076
  436.8 247.1 %copy-start.19 = (bf16[256,12,64]{0,2,1:T(8,128)(2,1)S(1)}, bf16[256,12,64]{0,2,1:T(8,128)(2,1)}, u32[]{:S(2)}) copy-start(bf16[256,12,64]{0,2,1:T(8,128)(2,1)} %copy-done.18) | copy-start | bytes 1179652
  436.8 254.0 %reduce-scatter.18.cloned.1.call-start = ((), (), s32[]{:S(2)}) async-start(), calls=%async_computation.17 | async-start | bytes 221184
  440.5 334.0 %all-reduce.19.cloned.1.call-start = ((), (), s32[]{:S(2)}) async-start(), calls=%async_computation.18 | async-start | bytes 3833856 | tf_op jit(solution)/shard_map/psum | solution.py:340
  (46 other events, 447.2 us)
Sparse Core Ops, SparseCore 0:
  9.9 36.5 all-gather.11
  50.7 32.3 all-gather.13
  85.6 32.1 all-gather.15
  119.5 23.9 all-gather.17
  145.2 38.7 all-gather.19
  185.8 38.7 all-gather.21
  226.5 32.1 all-gather.23
  260.6 32.3 all-gather.25
  422.4 76.2 reduce-scatter.15
  502.3 36.6 reduce-scatter.9
  542.5 53.7 reduce-scatter.11
  599.6 53.7 reduce-scatter.13
  657.1 33.6 reduce-scatter.17
  693.8 80.6 all-reduce.18
where the time goes:
time: 794 us; the launch traced here: 788 us
  waiting for transfers between devices  398 us (50%)
  matrix products  130 us (16%)
  blocking collectives  103 us (13%)
  local copies, waits for them, and re-layouts  79.1 us (10%)
  loops' own time  32.1 us (4%)
  other arithmetic  27.6 us (3%)
  between operations  16.9 us (2%)
    psum x1, waiting for transfers between devices, body(): lax.psum(shard_grads[0].astype(jnp.bfloat16), 'replica').astype(jnp.float32)  66.8 us
    unnamed x16, waiting for transfers between devices  63.4 us
    reduce_scatter x1, waiting for transfers between devices, body(): lax.psum_scatter(local_grads[6].astype(jnp.bfloat16), 'shard', scatter_di...  57.3 us
    reduce_scatter x1, waiting for transfers between devices, body(): lax.psum_scatter(local_grads[8].astype(jnp.bfloat16), 'shard', scatter_di...  57.1 us
    unnamed x2, blocking collectives  47.7 us
    all_gather x1, waiting for transfers between devices, body(): lax.all_gather(w_qkv, 'shard', axis=0, tiled=True)  38.5 us
    reduce_scatter x1, waiting for transfers between devices, body(): lax.psum_scatter(local_grads[2].astype(jnp.bfloat16), 'shard', scatter_di...  38.3 us
    all_gather x1, waiting for transfers between devices, body(): lax.all_gather(w_back, 'shard', axis=0, tiled=True)  28.4 us
  transfers between devices with their start and end apart: 14, of which 11 were waited for; matrix products, arithmetic and copies ran while one was open for 19% of the time, Pallas kernels for 0%

commit v1 on v0

--- a/solution.py
+++ b/solution.py
@@ -337,7 +337,9 @@
         ).astype(jnp.float32),
     )
     total_grads = (
-        lax.psum(shard_grads[0].astype(jnp.bfloat16), "replica").astype(jnp.float32),
+        jnp.sum(lax.all_gather(shard_grads[0].astype(jnp.bfloat16), "replica"), axis=0).astype(
+            jnp.float32
+        ),
         lax.psum(shard_grads[1].astype(jnp.bfloat16), "replica").astype(jnp.float32),
         lax.psum(shard_grads[2].astype(jnp.bfloat16), "replica").astype(jnp.float32),
         lax.psum(shard_grads[3].astype(jnp.bfloat16), "replica").astype(jnp.float32),

time: 794 us -> 658 us (0.83)
  waiting for transfers between devices: 398 us -> 261 us
    unnamed x16, waiting for transfers between devices: 63.4 us -> 4.89 us
    reduce_scatter x1, waiting for transfers between devices: 57.3 us -> 0.02 us  [body(): lax.psum_scatter(local_grads[6].astype(jnp.bfloat16), 'shard', scatter_di...]
    reduce_scatter x0 -> x1, waiting for transfers between devices: none -> 53.5 us  [body(): lax.psum_scatter(local_grads[0].astype(jnp.bfloat16), 'shard', scatter_di...]
    reduce_scatter x1, waiting for transfers between devices: 38.3 us -> 0.02 us  [body(): lax.psum_scatter(local_grads[2].astype(jnp.bfloat16), 'shard', scatter_di...]
    reduce_scatter x1, waiting for transfers between devices: 57.1 us -> 20.1 us  [body(): lax.psum_scatter(local_grads[8].astype(jnp.bfloat16), 'shard', scatter_di...]
    all_gather x0 -> x1, waiting for transfers between devices: none -> 35 us  [body(): lax.all_gather(shard_grads[0].astype(jnp.bfloat16), 'replica')]
    psum x1, waiting for transfers between devices: 66.8 us -> 46.8 us  [body(): lax.psum(shard_grads[2].astype(jnp.bfloat16), 'replica').astype(jnp.float32)]
    all_gather x1, waiting for transfers between devices: 16.2 us -> 4.09 us  [body(): query_piece = lax.all_gather(query, 'shard', axis=0, tiled=True)]
  transfers between devices with their start and end apart: 14 -> 15, of which waited for: 11 -> 10; matrix products, arithmetic and copies ran while one was open for 19% -> 35% of each run, Pallas kernels for 0% -> 0%
where the time goes in v1:
time: 658 us; the launch traced here: 652 us
  waiting for transfers between devices  261 us (40%)
  matrix products  132 us (20%)
  blocking collectives  105 us (16%)
  local copies, waits for them, and re-layouts  72.2 us (11%)
  other arithmetic  32.2 us (5%)
  loops' own time  31.6 us (5%)
  between operations  16.9 us (3%)
    reduce_scatter x1, waiting for transfers between devices, body(): lax.psum_scatter(local_grads[0].astype(jnp.bfloat16), 'shard', scatter_di...  53.5 us
    unnamed x2, blocking collectives  48.1 us
    psum x1, waiting for transfers between devices, body(): lax.psum(shard_grads[2].astype(jnp.bfloat16), 'replica').astype(jnp.float32)  46.8 us
    all_gather x1, waiting for transfers between devices, body(): lax.all_gather(w_qkv, 'shard', axis=0, tiled=True)  38.5 us
    all_gather x1, waiting for transfers between devices, body(): lax.all_gather(shard_grads[0].astype(jnp.bfloat16), 'replica')  35 us
    all_gather x1, waiting for transfers between devices, body(): lax.all_gather(w_back, 'shard', axis=0, tiled=True)  28.7 us
    dot_general x9, matrix products, masked_scores(): jnp.einsum('qhd,khd->hqk', query_heads, key_heads, preferred_element_type...  25.7 us
    all_gather x1, waiting for transfers between devices, body(): lax.all_gather(w_in, 'shard', axis=0, tiled=True)  25.6 us
  transfers between devices with their start and end apart: 15, of which 10 were waited for; matrix products, arithmetic and copies ran while one was open for 35% of the time, Pallas kernels for 0%

profile of v1, /device:TPU:0, one launch (start us, length us, event | category | flops | bytes accessed | tf_op | source)
XLA Modules:
  0.0 652.4 jit_solution(9521956484370203380)
XLA Ops:
  8.0 38.5 %all-gather.14.cloned.1.call-done = bf16[768,2304]{1,0:T(8,128)(2,1)} async-done(((bf16[96,2304]{1,0:T(8,128)(2,1)}), bf16[768,2304]{1,0:T(8,128)(2,1)}) %all-gather.14.cloned.1.call-update) | async-done | bytes 3538960 | tf_op jit(solution)/shard_map/all_gather | solution.py:74
  50.7 8.7 %all-gather.2 = bf16[8,96,2]{1,2,0:T(2,128)(2,1)S(1)} all-gather(bf16[1,96,2]{1,2,0:T(2,128)(2,1)S(1)} %bitcast.174), channel_id=1, replica_groups=mesh['shard'=8,'replica'=4] {'shard'}, dimensions={0}, use_global_device_ids=true | all-gather | bytes 3456 | tf_op jit(solution)/shard_map/all_gather | solution.py:76
  64.6 24.2 %all-reduce.14 = (bf16[768]{0:T(1024)(128)(2,1)S(1)}, bf16[768]{0:T(1024)(128)(2,1)S(1)}, bf16[768]{0:T(1024)(128)(2,1)S(1)}, bf16[768]{0:T(1024)(128)(2,1)S(1)}, bf16[768]{0:T(1024)(128)(2,1)S(1)}) all-reduce(bf16[768]{0:T(1024)(128)(2,1)S(1)} %dynamic-update-slice, ...), channel_id=1, replica_groups=mesh['shard'=8,'replica'=4] {'shard'}, use_global_device_ids=true, to_apply=%add | all-reduce | flops 3840 | bytes 15360
  97.0 9.8 %all-gather.1 = s32[8,1,256]{2,1,0:T(1,128)} all-gather(s32[1,1,256]{2,1,0:T(1,128)S(1)} %bitcast.170), channel_id=1, replica_groups=mesh['shard'=8,'replica'=4] {'shard'}, dimensions={0}, use_global_device_ids=true | all-gather | bytes 9216 | tf_op jit(solution)/shard_map/all_gather | solution.py:96
  122.0 32.9 %while.48 = (s32[]{:T(128)}, f32[12,256]{1,0:T(8,128)S(1)}, f32[12,256]{1,0:T(8,128)S(1)}, f32[256,12,64]{0,2,1:T(8,128)S(1)}, s32[2048]{0:T(1024)}, /*index=5*/...) while((s32[]{:T(128)}, f32[12,256]{1,0:T(8,128)S(1)}, ...), condition=%wide.region_5.6_spmd, body=%wide.region_0.5_spmd.sunk | while | flops 420488192 | bytes 26287476 | solution.py:130
  157.9 25.6 %all-gather.22.cloned.1.call-done = bf16[768,3072]{1,0:T(8,128)(2,1)} async-done(((bf16[96,3072]{1,0:T(8,128)(2,1)}), bf16[768,3072]{1,0:T(8,128)(2,1)}) %all-gather.22.cloned.1.call-update) | async-done | bytes 4718608 | tf_op jit(solution)/shard_map/all_gather | solution.py:143
  183.5 11.8 %multiply_convert_fusion.8 = (bf16[256,3072]{1,0:T(8,128)(2,1)}, f32[256,3072]{1,0:T(8,128)}, f32[256,3072]{1,0:T(8,128)}) fusion(f32[3072]{0:T(1024)S(1)} %bitcast.173, bf16[768,3072]{1,0:T(8,128)(2,1)} %all-gather.22.cloned.1.call-done, f32[256,768]{1,0:T(8,128)S(1)} %get-tuple-element.1189, f32[768]{0:T(1024)S(1)} %convert_element_type.211, ...), kind=kOutput, calls=%fused_computation.63 | convolution fusion | flops 1260847104 | bytes 13389824 | tf_op jit(solution)/shard_map/dot_general | solution.py:151
  195.3 28.7 %all-gather.24.cloned.1.call-done = bf16[3072,768]{1,0:T(8,128)(2,1)} async-done(((bf16[384,768]{1,0:T(8,128)(2,1)}), bf16[3072,768]{1,0:T(8,128)(2,1)}) %all-gather.24.cloned.1.call-update) | async-done | bytes 4718608 | tf_op jit(solution)/shard_map/all_gather | solution.py:145
  263.5 9.3 %all_gather.83 = f32[12,2048]{1,0:T(8,128)S(1)} all-gather(f32[12,256]{1,0:T(8,128)} %log_add_fusion), channel_id=1, replica_groups=mesh['shard'=8,'replica'=4] {'shard'}, dimensions={1}, use_global_device_ids=true | all-gather | bytes 110592 | tf_op jit(solution)/shard_map/all_gather | solution.py:227
  274.5 8.8 %all_gather.85 = f32[12,2048]{1,0:T(8,128)S(1)} all-gather(f32[12,256]{1,0:T(8,128)} %fusion.66), channel_id=1, replica_groups=mesh['shard'=8,'replica'=4] {'shard'}, dimensions={1}, use_global_device_ids=true | all-gather | bytes 110592 | tf_op jit(solution)/shard_map/all_gather | solution.py:228
  284.2 51.4 %while.49 = (s32[]{:T(128)}, f32[256,12,64]{0,2,1:T(8,128)}, s32[2048]{0:T(1024)}, s32[]{:T(128)}, s32[]{:T(128)}, /*index=5*/s32[256]{0:T(256)}, bf16[2048,768]...) while((s32[]{:T(128)}, f32[256,12,64]{0,2,1:T(8,128)}, ...), condition=%wide.region_17.18_spmd, body=%wide.region_14.17_spmd.sunk | while | flops 613941248 | bytes 20745584 | solution.py:225
  288.1 11.9 %conditional.7 = (f32[256,12,64]{0,2,1:T(8,128)}) conditional(s32[]{:T(128)} %convert_element_type.317, f32[256,12,64]{0,2,1:T(8,128)} %get-tuple-element.1513, (s32[256]{0:T(256)}, s32[512]{0:T(512)S(1)}, bf16[2048,768]{0,1:T(8,128)(2,1)}, s32[]{:T(128)}, bf16[256,12,64]{0,2,1:T(8,128)(2,1)S(1)}, /*index=5*/f32[12,256]{1,0:T(8,128)}, ...), branch_computations={%region_15.15_spmd, %region_16.16_spmd} | conditional | flops 613941248 | bytes 20741160 | solution.py:223
  304.0 11.9 %conditional.7 = (f32[256,12,64]{0,2,1:T(8,128)}) conditional(s32[]{:T(128)} %convert_element_type.317, f32[256,12,64]{0,2,1:T(8,128)} %get-tuple-element.1513, (s32[256]{0:T(256)}, s32[512]{0:T(512)S(1)}, bf16[2048,768]{0,1:T(8,128)(2,1)}, s32[]{:T(128)}, bf16[256,12,64]{0,2,1:T(8,128)(2,1)S(1)}, /*index=5*/f32[12,256]{1,0:T(8,128)}, ...), branch_computations={%region_15.15_spmd, %region_16.16_spmd} | conditional | flops 613941248 | bytes 20741160 | solution.py:223
  319.8 11.9 %conditional.7 = (f32[256,12,64]{0,2,1:T(8,128)}) conditional(s32[]{:T(128)} %convert_element_type.317, f32[256,12,64]{0,2,1:T(8,128)} %get-tuple-element.1513, (s32[256]{0:T(256)}, s32[512]{0:T(512)S(1)}, bf16[2048,768]{0,1:T(8,128)(2,1)}, s32[]{:T(128)}, bf16[256,12,64]{0,2,1:T(8,128)(2,1)S(1)}, /*index=5*/f32[12,256]{1,0:T(8,128)}, ...), branch_computations={%region_15.15_spmd, %region_16.16_spmd} | conditional | flops 613941248 | bytes 20741160 | solution.py:223
  342.4 68.2 %while.50 = (s32[]{:T(128)}, f32[256,12,64]{0,2,1:T(8,128)}, f32[256,12,64]{0,2,1:T(8,128)}, s32[2048]{0:T(1024)}, s32[]{:T(128)}, /*index=5*/s32[]{:T(128)}, s3...) while((s32[]{:T(128)}, f32[256,12,64]{0,2,1:T(8,128)}, ...), condition=%wide.region_21.22_spmd, body=%wide.region_18.21_spmd.sunk | while | flops 821755904 | bytes 29670792 | solution.py:275
  346.3 17.4 %conditional.8 = ((f32[256,12,64]{0,2,1:T(8,128)}, f32[256,12,64]{0,2,1:T(8,128)})) conditional(s32[]{:T(128)} %convert_element_type.318, (f32[256,12,64]{0,2,1:T(8,128)}, f32[256,12,64]{0,2,1:T(8,128)}) %tuple.170, (s32[512]{0:T(512)S(1)}, s32[256]{0:T(256)S(1)}, bf16[2048,768]{0,1:T(8,128)(2,1)}, s32[]{:T(128)}, ...), branch_computations={%region_19.19_spmd, %region_20.20_spmd} | conditional | flops 821755904 | bytes 29666336 | solution.py:273
  367.7 17.2 %conditional.8 = ((f32[256,12,64]{0,2,1:T(8,128)}, f32[256,12,64]{0,2,1:T(8,128)})) conditional(s32[]{:T(128)} %convert_element_type.318, (f32[256,12,64]{0,2,1:T(8,128)}, f32[256,12,64]{0,2,1:T(8,128)}) %tuple.170, (s32[512]{0:T(512)S(1)}, s32[256]{0:T(256)S(1)}, bf16[2048,768]{0,1:T(8,128)(2,1)}, s32[]{:T(128)}, ...), branch_computations={%region_19.19_spmd, %region_20.20_spmd} | conditional | flops 821755904 | bytes 29666336 | solution.py:273
  388.8 17.7 %conditional.8 = ((f32[256,12,64]{0,2,1:T(8,128)}, f32[256,12,64]{0,2,1:T(8,128)})) conditional(s32[]{:T(128)} %convert_element_type.318, (f32[256,12,64]{0,2,1:T(8,128)}, f32[256,12,64]{0,2,1:T(8,128)}) %tuple.170, (s32[512]{0:T(512)S(1)}, s32[256]{0:T(256)S(1)}, bf16[2048,768]{0,1:T(8,128)(2,1)}, s32[]{:T(128)}, ...), branch_computations={%region_19.19_spmd, %region_20.20_spmd} | conditional | flops 821755904 | bytes 29666336 | solution.py:273
  427.2 20.1 %reduce-scatter.14.cloned.1.call-done = bf16[384,768]{1,0:T(8,128)(2,1)} async-done(((bf16[3072,768]{1,0:T(8,128)(2,1)}), bf16[384,768]{1,0:T(8,128)(2,1)}) %reduce-scatter.14.cloned.1.call-update) | async-done | bytes 589840 | tf_op jit(solution)/shard_map/reduce_scatter | solution.py:326
  447.4 53.5 %reduce-scatter.16.cloned.1.call-done = bf16[96,2304]{1,0:T(8,128)(2,1)} async-done(((bf16[768,2304]{1,0:T(8,128)(2,1)}), bf16[96,2304]{1,0:T(8,128)(2,1)}) %reduce-scatter.16.cloned.1.call-update) | async-done | bytes 442384 | tf_op jit(solution)/shard_map/reduce_scatter | solution.py:302
  505.7 23.9 %all-reduce.13 = (bf16[768]{0:T(1024)(128)(2,1)S(1)}, bf16[768]{0:T(1024)(128)(2,1)S(1)}, bf16[768]{0:T(1024)(128)(2,1)S(1)}, bf16[768]{0:T(1024)(128)(2,1)S(1)}...) all-reduce(bf16[768]{0:T(1024)(128)(2,1)} %dynamic-update-slice.5, ...), channel_id=1, replica_groups=mesh['shard'=8,'replica'=4] {'shard'}, use_global_device_ids=true, to_apply=%add.5 | all-reduce | flops 8448 | bytes 33792
  539.0 11.9 %all-reduce.15 = (bf16[2,96]{1,0:T(2,128)(2,1)S(1)}, bf16[96]{0:T(256)(128)(2,1)S(1)}, bf16[96]{0:T(256)(128)(2,1)S(1)}, bf16[96]{0:T(256)(128)(2,1)S(1)}, bf16[...) all-reduce(bf16[2,96]{1,0:T(2,128)(2,1)S(1)} %copy.94, ...), channel_id=1, replica_groups=mesh['shard'=8,'replica'=4] {'replica'}, use_global_device_ids=true, to_apply=%region_27.28 | all-reduce | flops 1152 | bytes 4608 | tf_op jit(solution)/shard_map/psum | solution.py:343
  555.1 46.8 %all-reduce.19.cloned.1.call-done = (bf16[96,768]{1,0:T(8,128)(2,1)}, bf16[96,3072]{1,0:T(8,128)(2,1)}, bf16[384,768]{1,0:T(8,128)(2,1)}) async-done(((bf16[96,768]{1,0:T(8,128)(2,1)}, bf16[96,3072]{1,0:T(8,128)(2,1)}, bf16[384,768]{1,0:T(8,128)(2,1)}), (bf16[96,768]{1,0:T(8,128)(2,1)}, bf16[96,3072]{1,0:T(8,128)(2,1)}, bf16[384,768]{1,0:T(8,128)(2,1)})) %all-reduce.19.cloned.1.call-update) | async-done | bytes 1327120 | tf_op jit(solution)/shard_map/psum | solution.py:344
  607.9 35.0 %all-gather.30.cloned.1.call-done = bf16[384,2304]{1,0:T(8,128)(2,1)} async-done(((bf16[96,2304]{1,0:T(8,128)(2,1)}), bf16[384,2304]{1,0:T(8,128)(2,1)}) %all-gather.30.cloned.1.call-update) | async-done | bytes 1769488 | tf_op jit(solution)/shard_map/all_gather | solution.py:340
  (322 shorter events, 264.3 us)
Async XLA Ops:
  7.2 39.3 %all-gather.14.cloned.1.call-start = ((), (), s32[]{:S(2)}) async-start(), calls=%async_computation.5 | async-start | bytes 3981312 | tf_op jit(solution)/shard_map/all_gather | solution.py:74
  7.9 100.3 %all-gather.16.cloned.1.call-start = ((), (), s32[]{:S(2)}) async-start(), calls=%async_computation.6 | async-start | bytes 3538944 | tf_op jit(solution)/shard_map/all_gather | solution.py:94
  49.8 47.2 %copy-start.18 = (s32[256]{0:T(256)S(1)}, s32[256]{0:T(256)}, u32[]{:S(2)}) copy-start(s32[256]{0:T(256)} %param.28) | copy-start | bytes 3076
  50.6 66.6 %all-gather.18.cloned.1.call-start = ((), (), s32[]{:S(2)}) async-start(), calls=%async_computation.7 | async-start | bytes 3538944 | tf_op jit(solution)/shard_map/all_gather | solution.py:95
  60.4 94.6 %all-gather.20.cloned.1.call-start = ((), (), s32[]{:S(2)}) async-start(), calls=%async_computation.8 | async-start | bytes 1327104 | tf_op jit(solution)/shard_map/all_gather | solution.py:75
  61.0 122.5 %all-gather.22.cloned.1.call-start = ((), (), s32[]{:S(2)}) async-start(), calls=%async_computation.9 | async-start | bytes 5308416 | tf_op jit(solution)/shard_map/all_gather | solution.py:143
  61.6 162.5 %all-gather.24.cloned.1.call-start = ((), (), s32[]{:S(2)}) async-start(), calls=%async_computation.10 | async-start | bytes 5308416 | tf_op jit(solution)/shard_map/all_gather | solution.py:145
  62.1 196.0 %all-gather.26.cloned.1.call-start = ((), (), s32[]{:S(2)}) async-start(), calls=%async_computation.11 | async-start | bytes 3538944 | tf_op jit(solution)/shard_map/all_gather | solution.py:230
  96.9 127.1 %copy-start.23 = (f32[768]{0:T(1024)}, f32[768]{0:T(1024)S(1)}, u32[]{:S(2)}) copy-start(f32[768]{0:T(1024)S(1)} %convert_element_type.211) | copy-start | bytes 9220
  97.0 127.1 %copy-start.21 = (f32[768]{0:T(1024)}, f32[768]{0:T(1024)S(1)}, u32[]{:S(2)}) copy-start(f32[768]{0:T(1024)S(1)} %convert_element_type.210) | copy-start | bytes 9220
  97.0 131.8 %copy-start.25 = (f32[768]{0:T(1024)}, f32[768]{0:T(1024)S(1)}, u32[]{:S(2)}) copy-start(f32[768]{0:T(1024)S(1)} %convert_element_type.216) | copy-start | bytes 9220
  107.6 228.1 %all-gather.28.cloned.1.call-start = ((), (), s32[]{:S(2)}) async-start(), calls=%async_computation.12 | async-start | bytes 3538944 | tf_op jit(solution)/shard_map/all_gather | solution.py:231
  237.9 189.4 %reduce-scatter.10.cloned.1.call-start = ((), (), s32[]{:S(2)}) async-start(), calls=%async_computation.13 | async-start | bytes 1327104 | tf_op jit(solution)/shard_map/reduce_scatter | solution.py:308
  239.5 187.7 %reduce-scatter.12.cloned.1.call-start = ((), (), s32[]{:S(2)}) async-start(), calls=%async_computation.14 | async-start | bytes 5308416 | tf_op jit(solution)/shard_map/reduce_scatter | solution.py:320
  244.8 202.6 %reduce-scatter.14.cloned.1.call-start = ((), (), s32[]{:S(2)}) async-start(), calls=%async_computation.15 | async-start | bytes 5308416 | tf_op jit(solution)/shard_map/reduce_scatter | solution.py:326
  251.0 249.8 %reduce-scatter.16.cloned.1.call-start = ((), (), s32[]{:S(2)}) async-start(), calls=%async_computation.17 | async-start | bytes 3981312 | tf_op jit(solution)/shard_map/reduce_scatter | solution.py:302
  423.3 80.8 %copy-start.1 = (f32[256,768]{1,0:T(8,128)S(1)}, f32[256,768]{1,0:T(8,128)}, u32[]{:S(2)}) copy-start(f32[256,768]{1,0:T(8,128)} %copy-done) | copy-start | bytes 2359300
  423.3 80.8 %copy-start.30 = (f32[256]{0:T(256)S(1)}, f32[256]{0:T(256)}, u32[]{:S(2)}) copy-start(f32[256]{0:T(256)} %copy-done.29) | copy-start | bytes 3076
  423.3 80.9 %copy-start.6 = (f32[256,768]{1,0:T(8,128)S(1)}, f32[256,768]{1,0:T(8,128)}, u32[]{:S(2)}) copy-start(f32[256,768]{1,0:T(8,128)} %copy-done.4) | copy-start | bytes 2359300
  423.4 106.8 %copy-start.26 = (f32[768]{0:T(1024)S(1)}, f32[768]{0:T(1024)}, u32[]{:S(2)}) copy-start(f32[768]{0:T(1024)} %copy-done.25) | copy-start | bytes 9220
  423.4 106.8 %copy-start.28 = (f32[256]{0:T(256)S(1)}, f32[256]{0:T(256)}, u32[]{:S(2)}) copy-start(f32[256]{0:T(256)} %copy-done.27) | copy-start | bytes 3076
  423.4 114.8 %reduce-scatter.18.cloned.1.call-start = ((), (), s32[]{:S(2)}) async-start(), calls=%async_computation.18 | async-start | bytes 221184
  427.1 174.8 %all-reduce.19.cloned.1.call-start = ((), (), s32[]{:S(2)}) async-start(), calls=%async_computation.19 | async-start | bytes 2654208 | tf_op jit(solution)/shard_map/psum | solution.py:344
  447.3 195.5 %all-gather.30.cloned.1.call-start = ((), (), s32[]{:S(2)}) async-start(), calls=%async_computation.16 | async-start | bytes 2211840 | tf_op jit(solution)/shard_map/all_gather | solution.py:340
  (40 other events, 418.7 us)
Sparse Core Ops, SparseCore 0:
  9.9 36.5 all-gather.13
  50.7 32.3 all-gather.15
  85.0 32.1 all-gather.17
  118.9 23.9 all-gather.19
  144.6 38.7 all-gather.21
  185.2 38.7 all-gather.23
  225.9 32.1 all-gather.25
  260.0 32.3 all-gather.27
  296.2 36.6 reduce-scatter.9
  336.2 53.7 reduce-scatter.11
  393.5 53.7 reduce-scatter.13
  450.7 50.1 reduce-scatter.15
  504.5 33.6 reduce-scatter.17
  540.6 61.2 all-reduce.18
  603.3 39.4 all-gather.29
